TPU v7x, 32 devices: a whole 2x2x4 slice. The times are simulated.
32 devices in a mesh: dp: 16 (over z, y, core), seq: 2 (over x).
Axes of the slice: x: 2, y: 2, z: 4, core: 2. Of those that a mesh axis runs over, the one named last changes fastest.
Arguments:
- pre_act: bfloat16 [16, 512, 768], P('dp', 'seq'), may hold values from -6 to 6
- trunk_grad: bfloat16 [16, 256, 768], P('dp', None, 'seq'), may hold values from -6 to 6
- conv_weight: bfloat16 [5, 768, 768], P(None, 'dp'), may hold values from -0.09375 to 0.09375
- pair_weight: bfloat16 [768, 768], replicated, may hold values from -0.21875 to 0.21875
- donor_slots: int32 [16, 2, 2, 128], P('dp', 'seq'), may hold values from 0 to 255
- accept_slots: int32 [16, 2, 2, 128], P('dp', 'seq'), may hold values from 0 to 255
- junction_grad: float32 [16, 2, 2, 128], P('dp', 'seq'), may hold values from -6 to 6
- pair_counts: int32 [16, 2, 2], P('dp'), may hold values from 0 to 128, as said below
Outputs:
- input_grad: bfloat16 [16, 512, 768], P('dp', 'seq')
- pair_grad: float32 [768, 768], replicated
Inputs may be any that keep to these rules, and one draw needn't show every extreme that they name: pair_counts is at most 128; in every sample some acceptor slab has 128 live slots from every donor slab.
All inputs are finite; a program needn't handle non-finite values.
Results may differ from a plain program's by a relative error of at most 0.0061.
Values may be sent and summed in bfloat16 or wider, within the bound.
A program may use at most 64 MiB of HBM per device.

v0:
```python
import math
import jax
import jax.numpy as jnp
from jax import lax
from jax.sharding import PartitionSpec as P


def with_halo(x, sides, width):
    for axis, dim in sides:
        size, length = (lax.axis_size(axis), x.shape[dim])
        up = [(i, (i + 1) % size) for i in range(size - 1)]
        down = [(j, i) for i, j in up]
        last = lax.slice_in_dim(x, length - width, length, axis=dim)
        first = lax.slice_in_dim(x, 0, width, axis=dim)
        before = lax.ppermute(last, axis, up)
        after = lax.ppermute(first, axis, down)
        x = jnp.concatenate([before, x, after], axis=dim)
    return x


def gelu_parts(values):
    normal_cdf = 0.5 * (1.0 + jax.scipy.special.erf(values / math.sqrt(2.0)))
    density = jnp.exp(-0.5 * values * values) / math.sqrt(2.0 * math.pi)
    return (values * normal_cdf, normal_cdf + values * density)


def per_device(
    pre_act,
    trunk_grad,
    conv_weight,
    pair_weight,
    donor_slots,
    accept_slots,
    junction_grad,
    pair_counts,
):
    seq_count = lax.axis_size("seq")
    my_slab = lax.axis_index("seq")
    slab_len = pre_act.shape[1]
    channels = pre_act.shape[2]
    slot_count = donor_slots.shape[3]
    kernel = conv_weight.shape[0]
    half = kernel // 2
    act_f, slope = gelu_parts(pre_act[0].astype(jnp.float32))
    act = act_f.astype(jnp.bfloat16)
    arrived = lax.all_to_all(trunk_grad, "seq", split_axis=1, concat_axis=2, tiled=True)
    pooled = jnp.repeat(arrived[0].astype(jnp.float32) * 0.5, 2, axis=0)
    send_index = donor_slots[0, 0].reshape(-1)
    outgoing = act[send_index].reshape(seq_count, slot_count, channels)
    incoming = lax.all_to_all(outgoing, "seq", split_axis=0, concat_axis=0, tiled=True)
    donor_rows = incoming.reshape(-1, channels)
    accept_index = accept_slots[0, 0].reshape(-1)
    counts_in = lax.dynamic_index_in_dim(pair_counts[0], my_slab, axis=1, keepdims=False)
    live = jnp.arange(slot_count, dtype=jnp.int32)[None, :] < counts_in[:, None]
    slot_w = jnp.where(live, junction_grad[0, 0], 0.0).reshape(-1)
    accept_rows = act[accept_index]
    weighted = (slot_w[:, None] * accept_rows.astype(jnp.float32)).astype(jnp.bfloat16)
    accept_term = (
        jnp.dot(donor_rows, pair_weight, preferred_element_type=jnp.float32) * slot_w[:, None]
    )
    donor_term = lax.dot_general(
        weighted, pair_weight, (((1,), (1,)), ((), ())), preferred_element_type=jnp.float32
    ).astype(jnp.bfloat16)
    pair_part = lax.dot_general(
        donor_rows, weighted, (((0,), (0,)), ((), ())), preferred_element_type=jnp.float32
    )
    returned = lax.all_to_all(
        donor_term.reshape(seq_count, slot_count, channels),
        "seq",
        split_axis=0,
        concat_axis=0,
        tiled=True,
    )
    act_grad = (
        pooled.at[accept_index]
        .add(accept_term)
        .at[send_index]
        .add(returned.reshape(-1, channels).astype(jnp.float32))
    )
    conv_grad = (act_grad * slope).astype(jnp.bfloat16)
    padded = with_halo(conv_grad[None], (("seq", 1),), half)[0]
    piece = lax.all_gather(conv_weight, "dp", axis=1, tiled=True)
    total = jnp.zeros((slab_len, piece.shape[1]), jnp.float32)
    for tap in range(kernel):
        window = padded[2 * half - tap : 2 * half - tap + slab_len]
        total = total + lax.dot_general(
            window, piece[tap], (((1,), (1,)), ((), ())), preferred_element_type=jnp.float32
        )
    input_grad = total.astype(jnp.bfloat16)
    pair_sum = lax.psum(pair_part, ("dp", "seq"))
    scale = 1.0 / math.sqrt(lax.axis_size("dp") * seq_count * seq_count * slot_count)
    return (input_grad[None], pair_sum * scale)


def solution(mesh):
    in_specs = (
        P("dp", "seq", None),
        P("dp", None, "seq"),
        P(None, "dp", None),
        P(),
        P("dp", "seq", None, None),
        P("dp", "seq", None, None),
        P("dp", "seq", None, None),
        P("dp", None, None),
    )
    out_specs = (P("dp", "seq", None), P())
    return jax.shard_map(
        per_device, mesh=mesh, in_specs=in_specs, out_specs=out_specs, check_vma=False
    )
```

profile of v0, /device:TPU:0, one launch (start us, length us, event | category | flops | bytes accessed | tf_op | source)
XLA Modules:
  0.0 200.0 jit_solution(1862598864620470224)
XLA Ops:
  8.0 1.3 fusion.6
  9.3 0.7 compare_select_fusion
  10.0 1.9 gather_fusion
  11.9 4.3 %all-to-all-start.1 = ((bf16[2,128,768]{2,1,0:T(8,128)(2,1)}), bf16[2,128,768]{2,1,0:T(8,128)(2,1)S(1)}, u32[]{:S(2)}, u32[]{:S(2)}) async-start(bf16[2,128,768]{2,1,0:T(8,128)(2,1)} %bitcast.9), calls=%async_computation.1 | async-start | bytes 786432 | tf_op jit(solution)/shard_map/all_to_all | solution.py:50
  16.3 1.2 gather_fusion.1
  17.8 5.8 %all-to-all-done.1 = bf16[2,128,768]{2,1,0:T(8,128)(2,1)S(1)} async-done(((bf16[2,128,768]{2,1,0:T(8,128)(2,1)}), bf16[2,128,768]{2,1,0:T(8,128)(2,1)S(1)}, u32[]{:S(2)}, u32[]{:S(2)}) %all-to-all-start.1) | async-done | bytes 393248 | tf_op jit(solution)/shard_map/all_to_all | solution.py:50
  23.6 2.0 fusion.26
  25.6 0.5 all-gather.2.cloned.1.call-update
  26.2 0.3 copy.19
  26.5 0.5 broadcast.65
  27.0 1.8 reduce.2
  28.8 0.7 reshape.152
  29.5 3.4 %all-to-all-start = ((bf16[2,2,24576]{2,1,0:T(2,128)(2,1)}), bf16[2,2,24576]{2,1,0:T(2,128)(2,1)S(1)}, u32[]{:S(2)}, u32[]{:S(2)}) async-start(bf16[2,2,24576]{2,1,0:T(2,128)(2,1)} %reshape.152), calls=%async_computation | async-start | bytes 393216 | tf_op jit(solution)/shard_map/all_to_all | solution.py:46
  33.0 1.3 convolution_convert_fusion
  34.3 4.3 %all-to-all-done = bf16[2,2,24576]{2,1,0:T(2,128)(2,1)S(1)} async-done(((bf16[2,2,24576]{2,1,0:T(2,128)(2,1)}), bf16[2,2,24576]{2,1,0:T(2,128)(2,1)S(1)}, u32[]{:S(2)}, u32[]{:S(2)}) %all-to-all-start) | async-done | bytes 196640 | tf_op jit(solution)/shard_map/all_to_all | solution.py:46
  38.6 4.2 %all-to-all-start.2 = ((bf16[2,128,768]{2,1,0:T(8,128)(2,1)}), bf16[2,128,768]{2,1,0:T(8,128)(2,1)}, u32[]{:S(2)}, u32[]{:S(2)}) async-start(bf16[2,128,768]{2,1,0:T(8,128)(2,1)} %bitcast.13), calls=%async_computation.2 | async-start | bytes 786432 | tf_op jit(solution)/shard_map/all_to_all | solution.py:67
  43.4 0.3 broadcast_in_dim.10
  43.7 0.5 reshape.111
  44.2 0.5 convolution_multiply_fusion
  44.7 2.5 %scatter_fusion = f32[256,768]{1,0:T(8,128)S(1)} fusion(f32[256,768]{1,0:T(8,128)S(1)} %reshape.111, s32[256]{0:T(256)S(1)} %bitcast.77, f32[256,768]{1,0:T(8,128)S(1)} %convolution_multiply_fusion), kind=kCustom, calls=%fused_computation.2 | custom fusion | flops 196608 | bytes 2360320 | tf_op jit(solution)/shard_map/scatter-add | solution.py:76
  47.3 2.6 %all-to-all-done.2 = bf16[2,128,768]{2,1,0:T(8,128)(2,1)} async-done(((bf16[2,128,768]{2,1,0:T(8,128)(2,1)}), bf16[2,128,768]{2,1,0:T(8,128)(2,1)}, u32[]{:S(2)}, u32[]{:S(2)}) %all-to-all-start.2) | async-done | bytes 393248 | tf_op jit(solution)/shard_map/all_to_all | solution.py:67
  49.9 3.0 %scatter_custom_fusion.1 = f32[256,768]{1,0:T(8,128)S(1)} fusion(f32[256,768]{1,0:T(8,128)S(1)} %scatter_fusion, s32[256]{0:T(256)S(1)} %bitcast.79, bf16[256,768]{1,0:T(8,128)(2,1)} %bitcast.27), kind=kCustom, calls=%fused_computation.33 | custom fusion | flops 393216 | bytes 1179648 | tf_op jit(solution)/shard_map/scatter-add | solution.py:78
  52.9 0.4 fusion.11
  53.3 1.3 collective-permute-start
  54.6 4.7 %collective-permute-start.1 = (bf16[1,2,768]{2,1,0:T(2,128)(2,1)S(1)}, bf16[1,2,768]{2,1,0:T(2,128)(2,1)S(1)}, u32[]{:S(2)}, u32[]{:S(2)}) collective-permute-start(bf16[1,2,768]{2,1,0:T(2,128)(2,1)S(1)} %get-tuple-element.2), channel_id=1, source_target_pairs={{0,1},{2,3},{4,5},{6,7},{8,9},{10,11},{12,13},{14,15},{16,17},{18,... | collective-permute-start | bytes 9224 | tf_op jit(solution)/shard_map/ppermute | solution.py:15
  59.3 123.8 %all-reduce.2.cloned.1.call-done = f32[768,768]{1,0:T(8,128)} async-done(((f32[768,768]{1,0:T(8,128)}), f32[768,768]{1,0:T(8,128)}) %all-reduce.2.cloned.1.call-update) | async-done | bytes 2359312 | tf_op jit(solution)/shard_map/psum | solution.py:90
  183.1 3.3 %broadcast_multiply_fusion = f32[768,768]{1,0:T(8,128)} fusion(f32[768,768]{1,0:T(8,128)} %all-reduce.2.cloned.1.call-done), kind=kLoop, calls=%fused_computation.23 | loop fusion | flops 589824 | bytes 4718592 | tf_op jit(solution)/shard_map/mul | solution.py:92
  186.4 1.9 fusion.2
  188.3 1.9 convolution_add_fusion.3
  190.3 0.5 convolution_add_fusion.2
  190.8 0.5 convolution_add_fusion.1
  191.3 1.3 fusion.1
  (30 shorter events, 1.0 us)
Async XLA Ops:
  8.0 25.0 %copy-start = (bf16[768,768]{1,0:T(8,128)(2,1)S(1)}, bf16[768,768]{1,0:T(8,128)(2,1)}, u32[]{:S(2)}) copy-start(bf16[768,768]{1,0:T(8,128)(2,1)} %param.11) | copy-start | bytes 3538948
  9.3 7.0 %copy-start.4 = (s32[1,1,2,128]{3,2,1,0:T(2,128)S(1)}, s32[1,1,2,128]{3,2,1,0:T(2,128)}, u32[]{:S(2)}) copy-start(s32[1,1,2,128]{3,2,1,0:T(2,128)} %param.13) | copy-start | bytes 3076
  11.9 5.6 %copy-start.5 = (s32[1,2,2]{2,1,0:T(2,128)S(1)}, s32[1,2,2]{2,1,0:T(2,128)}, u32[]{:S(2)}) copy-start(s32[1,2,2]{2,1,0:T(2,128)} %param.15) | copy-start | bytes 52
  11.9 5.8 %copy-start.6 = (f32[1,1,2,128]{3,2,1,0:T(2,128)S(1)}, f32[1,1,2,128]{3,2,1,0:T(2,128)}, u32[]{:S(2)}) copy-start(f32[1,1,2,128]{3,2,1,0:T(2,128)} %param.14) | copy-start | bytes 3076
  11.9 11.6 %all-to-all-start.1 = ((bf16[2,128,768]{2,1,0:T(8,128)(2,1)}), bf16[2,128,768]{2,1,0:T(8,128)(2,1)S(1)}, u32[]{:S(2)}, u32[]{:S(2)}) async-start(bf16[2,128,768]{2,1,0:T(8,128)(2,1)} %bitcast.9), calls=%async_computation.1 | async-start | bytes 786432 | tf_op jit(solution)/shard_map/all_to_all | solution.py:50
  16.3 166.8 %all-reduce.2.cloned.1.call-start = ((), (), s32[]{:S(2)}) async-start(), calls=%async_computation.4 | async-start | bytes 4718592 | tf_op jit(solution)/shard_map/psum | solution.py:90
  23.6 2.6 %copy-start.3 = (bf16[1,256,384]{2,1,0:T(8,128)(2,1)S(1)}, bf16[1,256,384]{2,1,0:T(8,128)(2,1)}, u32[]{:S(2)}) copy-start(bf16[1,256,384]{2,1,0:T(8,128)(2,1)} %param.9) | copy-start | bytes 589828
  25.6 160.8 %all-gather.2.cloned.1.call-start = ((), (), s32[]{:S(2)}) async-start(), calls=%async_computation.3 | async-start | bytes 6266880 | tf_op jit(solution)/shard_map/all_gather | solution.py:82
  29.5 9.0 %all-to-all-start = ((bf16[2,2,24576]{2,1,0:T(2,128)(2,1)}), bf16[2,2,24576]{2,1,0:T(2,128)(2,1)S(1)}, u32[]{:S(2)}, u32[]{:S(2)}) async-start(bf16[2,2,24576]{2,1,0:T(2,128)(2,1)} %reshape.152), calls=%async_computation | async-start | bytes 393216 | tf_op jit(solution)/shard_map/all_to_all | solution.py:46
  38.6 11.3 %all-to-all-start.2 = ((bf16[2,128,768]{2,1,0:T(8,128)(2,1)}), bf16[2,128,768]{2,1,0:T(8,128)(2,1)}, u32[]{:S(2)}, u32[]{:S(2)}) async-start(bf16[2,128,768]{2,1,0:T(8,128)(2,1)} %bitcast.13), calls=%async_computation.2 | async-start | bytes 786432 | tf_op jit(solution)/shard_map/all_to_all | solution.py:67
  44.7 8.2 %copy-start.1 = (bf16[1,256,768]{2,1,0:T(8,128)(2,1)S(1)}, bf16[1,256,768]{2,1,0:T(8,128)(2,1)}, u32[]{:S(2)}) copy-start(bf16[1,256,768]{2,1,0:T(8,128)(2,1)} %param.8) | copy-start | bytes 1179652
  53.3 133.1 %collective-permute-start = (bf16[1,2,768]{2,1,0:T(2,128)(2,1)S(1)}, bf16[1,2,768]{2,1,0:T(2,128)(2,1)S(1)}, u32[]{:S(2)}, u32[]{:S(2)}) collective-permute-start(bf16[1,2,768]{2,1,0:T(2,128)(2,1)S(1)} %get-tuple-element.3), channel_id=1, source_target_pairs={{1,0},{3,2},{5,4},{7,6},{9,8},{11,10},{13,12},{15,14},{17,16},{19,... | collective-permute-start | bytes 9224 | tf_op jit(solution)/shard_map/ppermute | solution.py:16
  54.6 136.2 %collective-permute-start.1 = (bf16[1,2,768]{2,1,0:T(2,128)(2,1)S(1)}, bf16[1,2,768]{2,1,0:T(2,128)(2,1)S(1)}, u32[]{:S(2)}, u32[]{:S(2)}) collective-permute-start(bf16[1,2,768]{2,1,0:T(2,128)(2,1)S(1)} %get-tuple-element.2), channel_id=1, source_target_pairs={{0,1},{2,3},{4,5},{6,7},{8,9},{10,11},{12,13},{14,15},{16,17},{18,... | collective-permute-start | bytes 9224 | tf_op jit(solution)/shard_map/ppermute | solution.py:15
  186.4 3.9 %copy-start.2 = (bf16[5,768,768]{2,1,0:T(8,128)(2,1)S(1)}, bf16[5,768,768]{2,1,0:T(8,128)(2,1)}, u32[]{:S(2)}) copy-start(bf16[5,768,768]{2,1,0:T(8,128)(2,1)} %all-gather.2.cloned.1.call-done) | copy-start | bytes 17694724
Sparse Core Ops, SparseCore 0:
  25.7 157.3 all-reduce.1
Sparse Core Ops, SparseCore 1:
  28.3 64.0 all-gather.1
where the time goes:
time: 200 us
  waiting for transfers between devices  137 us (68%)
  starting transfers between devices  18 us (9%)
  between operations  15.7 us (8%)
  other arithmetic  13.1 us (7%)
  matrix products  9.85 us (5%)
  local copies, waits for them, and re-layouts  6.27 us (3%)
    psum x1, waiting for transfers between devices, per_device(): pair_sum = lax.psum(pair_part, ('dp', 'seq'))  124 us
    dot_general x5, matrix products, per_device(): lax.dot_general(window, piece[tap], (((1,), (1,)), ((), ())), preferred_e...  6.13 us
    all_to_all x1, waiting for transfers between devices, per_device(): lax.all_to_all(outgoing, 'seq', split_axis=0, concat_axis=0, tiled=True)  5.81 us
    scatter-add x2, other arithmetic, per_device(): act_grad = pooled.at[accept_index].add(accept_term).at[send_index].add(re...  5.57 us
    ppermute x1, starting transfers between devices, with_halo(): before = lax.ppermute(last, axis, up)  4.72 us
    all_to_all x1, starting transfers between devices, per_device(): lax.all_to_all(outgoing, 'seq', split_axis=0, concat_axis=0, tiled=True)  4.34 us
    all_to_all x1, waiting for transfers between devices, per_device(): lax.all_to_all(trunk_grad, 'seq', split_axis=1, concat_axis=2, tiled=True)  4.32 us
    all_to_all x1, starting transfers between devices, per_device(): lax.all_to_all(donor_term.reshape(seq_count, slot_count, channels), 'seq'...  4.17 us
  transfers between devices with their start and end apart: 7, of which 4 were waited for; matrix products, arithmetic and copies ran while one was open for 11% of the time, Pallas kernels for 0%

commit v1 on v0

--- a/solution.py
+++ b/solution.py
@@ -43,7 +43,10 @@
     half = kernel // 2
     act_f, slope = gelu_parts(pre_act[0].astype(jnp.float32))
     act = act_f.astype(jnp.bfloat16)
-    arrived = lax.all_to_all(trunk_grad, "seq", split_axis=1, concat_axis=2, tiled=True)
+    arrived = jnp.concatenate(
+        lax.all_to_all(jnp.stack(jnp.split(trunk_grad, lax.axis_size("seq"), axis=1)), "seq", 0, 0),
+        axis=2,
+    )
     pooled = jnp.repeat(arrived[0].astype(jnp.float32) * 0.5, 2, axis=0)
     send_index = donor_slots[0, 0].reshape(-1)
     outgoing = act[send_index].reshape(seq_count, slot_count, channels)

time: 200 us -> 200 us (level)
  waiting for transfers between devices: 137 us -> 140 us
    psum x1, waiting for transfers between devices: 124 us -> 127 us  [per_device(): pair_sum = lax.psum(pair_part, ('dp', 'seq'))]
  transfers between devices with their start and end apart: 7 -> 7, of which waited for: 4 -> 4; matrix products, arithmetic and copies ran while one was open for 11% -> 9% of each run, Pallas kernels for 0% -> 0%
where the time goes in v1:
time: 200 us
  waiting for transfers between devices  140 us (70%)
  starting transfers between devices  17.8 us (9%)
  between operations  15.7 us (8%)
  other arithmetic  12 us (6%)
  matrix products  9.85 us (5%)
  local copies, waits for them, and re-layouts  4.6 us (2%)
    psum x1, waiting for transfers between devices, per_device(): pair_sum = lax.psum(pair_part, ('dp', 'seq'))  127 us
    dot_general x5, matrix products, per_device(): lax.dot_general(window, piece[tap], (((1,), (1,)), ((), ())), preferred_e...  6.13 us
    all_to_all x1, waiting for transfers between devices, per_device(): lax.all_to_all(outgoing, 'seq', split_axis=0, concat_axis=0, tiled=True)  5.81 us
    scatter-add x2, other arithmetic, per_device(): act_grad = pooled.at[accept_index].add(accept_term).at[send_index].add(re...  5.58 us
    ppermute x1, starting transfers between devices, with_halo(): before = lax.ppermute(last, axis, up)  4.54 us
    all_to_all x1, waiting for transfers between devices, per_device(): lax.all_to_all(jnp.stack(jnp.split(trunk_grad, lax.axis_size('seq'), axis...  4.52 us
    all_to_all x1, starting transfers between devices, per_device(): lax.all_to_all(outgoing, 'seq', split_axis=0, concat_axis=0, tiled=True)  4.34 us
    all_to_all x1, starting transfers between devices, per_device(): lax.all_to_all(donor_term.reshape(seq_count, slot_count, channels), 'seq'...  4.15 us
  transfers between devices with their start and end apart: 7, of which 4 were waited for; matrix products, arithmetic and copies ran while one was open for 9% of the time, Pallas kernels for 0%

profile of v1, /device:TPU:0, one launch (start us, length us, event | category | flops | bytes accessed | tf_op | source)
XLA Modules:
  0.0 199.7 jit_solution(14936559200213618644)
XLA Ops:
  8.0 1.3 fusion.6
  9.3 0.7 compare_select_fusion
  10.0 1.9 gather_fusion
  11.9 4.3 %all-to-all-start.1 = ((bf16[2,128,768]{2,1,0:T(8,128)(2,1)}), bf16[2,128,768]{2,1,0:T(8,128)(2,1)S(1)}, u32[]{:S(2)}, u32[]{:S(2)}) async-start(bf16[2,128,768]{2,1,0:T(8,128)(2,1)} %bitcast.11), calls=%async_computation.1 | async-start | bytes 786432 | tf_op jit(solution)/shard_map/all_to_all | solution.py:53
  16.3 1.2 gather_fusion.1
  17.5 0.2 dynamic-slice_reduce_fusion
  17.8 5.8 %all-to-all-done.1 = bf16[2,128,768]{2,1,0:T(8,128)(2,1)S(1)} async-done(((bf16[2,128,768]{2,1,0:T(8,128)(2,1)}), bf16[2,128,768]{2,1,0:T(8,128)(2,1)S(1)}, u32[]{:S(2)}, u32[]{:S(2)}) %all-to-all-start.1) | async-done | bytes 393248 | tf_op jit(solution)/shard_map/all_to_all | solution.py:53
  23.6 2.0 fusion.26
  25.6 0.5 all-gather.2.cloned.1.call-update
  26.3 0.1 copy.18
  26.5 0.7 pad_maximum_fusion.2
  27.1 3.4 %all-to-all-start = ((bf16[2,1,128,384]{2,3,1,0:T(8,128)(2,1)}), bf16[2,1,128,384]{2,3,1,0:T(8,128)(2,1)S(1)}, u32[]{:S(2)}, u32[]{:S(2)}) async-start(bf16[2,1,128,384]{2,3,1,0:T(8,128)(2,1)} %pad_maximum_fusion.2), calls=%async_computation | async-start | bytes 393216 | tf_op jit(solution)/shard_map/all_to_all | solution.py:47
  30.6 1.3 convolution_convert_fusion
  31.9 4.5 %all-to-all-done = bf16[2,1,128,384]{2,3,1,0:T(8,128)(2,1)S(1)} async-done(((bf16[2,1,128,384]{2,3,1,0:T(8,128)(2,1)}), bf16[2,1,128,384]{2,3,1,0:T(8,128)(2,1)S(1)}, u32[]{:S(2)}, u32[]{:S(2)}) %all-to-all-start) | async-done | bytes 196640 | tf_op jit(solution)/shard_map/all_to_all | solution.py:47
  36.4 4.2 %all-to-all-start.2 = ((bf16[2,128,768]{2,1,0:T(8,128)(2,1)}), bf16[2,128,768]{2,1,0:T(8,128)(2,1)}, u32[]{:S(2)}, u32[]{:S(2)}) async-start(bf16[2,128,768]{2,1,0:T(8,128)(2,1)} %bitcast.15), calls=%async_computation.2 | async-start | bytes 786432 | tf_op jit(solution)/shard_map/all_to_all | solution.py:70
  40.6 0.2 copy.16
  40.8 0.3 broadcast_in_dim.10
  41.0 0.5 reshape.108
  41.6 0.5 convolution_multiply_fusion
  42.1 2.5 %scatter_fusion = f32[256,768]{1,0:T(8,128)S(1)} fusion(f32[256,768]{1,0:T(8,128)S(1)} %reshape.108, s32[256]{0:T(256)S(1)} %bitcast.75, f32[256,768]{1,0:T(8,128)S(1)} %convolution_multiply_fusion), kind=kCustom, calls=%fused_computation.2 | custom fusion | flops 196608 | bytes 2360320 | tf_op jit(solution)/shard_map/scatter-add | solution.py:79
  44.6 1.9 all-to-all-done.2
  46.5 3.0 %scatter_custom_fusion.1 = f32[256,768]{1,0:T(8,128)S(1)} fusion(f32[256,768]{1,0:T(8,128)S(1)} %scatter_fusion, s32[256]{0:T(256)S(1)} %bitcast.77, bf16[256,768]{1,0:T(8,128)(2,1)} %bitcast.29), kind=kCustom, calls=%fused_computation.33 | custom fusion | flops 393216 | bytes 1179648 | tf_op jit(solution)/shard_map/scatter-add | solution.py:81
  49.6 0.4 fusion.11
  49.9 1.3 collective-permute-start
  51.2 4.5 %collective-permute-start.1 = (bf16[1,2,768]{2,1,0:T(2,128)(2,1)S(1)}, bf16[1,2,768]{2,1,0:T(2,128)(2,1)S(1)}, u32[]{:S(2)}, u32[]{:S(2)}) collective-permute-start(bf16[1,2,768]{2,1,0:T(2,128)(2,1)S(1)} %get-tuple-element.2), channel_id=1, source_target_pairs={{0,1},{2,3},{4,5},{6,7},{8,9},{10,11},{12,13},{14,15},{16,17},{18,... | collective-permute-start | bytes 9224 | tf_op jit(solution)/shard_map/ppermute | solution.py:15
  55.8 127.0 %all-reduce.2.cloned.1.call-done = f32[768,768]{1,0:T(8,128)} async-done(((f32[768,768]{1,0:T(8,128)}), f32[768,768]{1,0:T(8,128)}) %all-reduce.2.cloned.1.call-update) | async-done | bytes 2359312 | tf_op jit(solution)/shard_map/psum | solution.py:93
  182.8 3.3 %broadcast_multiply_fusion = f32[768,768]{1,0:T(8,128)} fusion(f32[768,768]{1,0:T(8,128)} %all-reduce.2.cloned.1.call-done), kind=kLoop, calls=%fused_computation.23 | loop fusion | flops 589824 | bytes 4718592 | tf_op jit(solution)/shard_map/mul | solution.py:95
  186.1 1.9 fusion.2
  188.0 1.9 convolution_add_fusion.3
  190.0 0.5 convolution_add_fusion.2
  190.5 0.5 convolution_add_fusion.1
  191.0 1.3 fusion.1
  (28 shorter events, 0.4 us)
Async XLA Ops:
  8.0 22.6 %copy-start = (bf16[768,768]{1,0:T(8,128)(2,1)S(1)}, bf16[768,768]{1,0:T(8,128)(2,1)}, u32[]{:S(2)}) copy-start(bf16[768,768]{1,0:T(8,128)(2,1)} %param.11) | copy-start | bytes 3538948
  9.3 7.0 %copy-start.4 = (s32[1,1,2,128]{3,2,1,0:T(2,128)S(1)}, s32[1,1,2,128]{3,2,1,0:T(2,128)}, u32[]{:S(2)}) copy-start(s32[1,1,2,128]{3,2,1,0:T(2,128)} %param.13) | copy-start | bytes 3076
  11.9 5.6 %copy-start.5 = (s32[1,2,2]{2,1,0:T(2,128)S(1)}, s32[1,2,2]{2,1,0:T(2,128)}, u32[]{:S(2)}) copy-start(s32[1,2,2]{2,1,0:T(2,128)} %param.15) | copy-start | bytes 52
  11.9 5.8 %copy-start.6 = (f32[1,1,2,128]{3,2,1,0:T(2,128)S(1)}, f32[1,1,2,128]{3,2,1,0:T(2,128)}, u32[]{:S(2)}) copy-start(f32[1,1,2,128]{3,2,1,0:T(2,128)} %param.14) | copy-start | bytes 3076
  11.9 11.6 %all-to-all-start.1 = ((bf16[2,128,768]{2,1,0:T(8,128)(2,1)}), bf16[2,128,768]{2,1,0:T(8,128)(2,1)S(1)}, u32[]{:S(2)}, u32[]{:S(2)}) async-start(bf16[2,128,768]{2,1,0:T(8,128)(2,1)} %bitcast.11), calls=%async_computation.1 | async-start | bytes 786432 | tf_op jit(solution)/shard_map/all_to_all | solution.py:53
  16.3 166.6 %all-reduce.2.cloned.1.call-start = ((), (), s32[]{:S(2)}) async-start(), calls=%async_computation.4 | async-start | bytes 4718592 | tf_op jit(solution)/shard_map/psum | solution.py:93
  23.6 2.6 %copy-start.3 = (bf16[1,256,384]{2,1,0:T(8,128)(2,1)S(1)}, bf16[1,256,384]{2,1,0:T(8,128)(2,1)}, u32[]{:S(2)}) copy-start(bf16[1,256,384]{2,1,0:T(8,128)(2,1)} %param.9) | copy-start | bytes 589828
  25.6 160.5 %all-gather.2.cloned.1.call-start = ((), (), s32[]{:S(2)}) async-start(), calls=%async_computation.3 | async-start | bytes 6266880 | tf_op jit(solution)/shard_map/all_gather | solution.py:85
  27.1 9.2 %all-to-all-start = ((bf16[2,1,128,384]{2,3,1,0:T(8,128)(2,1)}), bf16[2,1,128,384]{2,3,1,0:T(8,128)(2,1)S(1)}, u32[]{:S(2)}, u32[]{:S(2)}) async-start(bf16[2,1,128,384]{2,3,1,0:T(8,128)(2,1)} %pad_maximum_fusion.2), calls=%async_computation | async-start | bytes 393216 | tf_op jit(solution)/shard_map/all_to_all | solution.py:47
  36.4 10.1 %all-to-all-start.2 = ((bf16[2,128,768]{2,1,0:T(8,128)(2,1)}), bf16[2,128,768]{2,1,0:T(8,128)(2,1)}, u32[]{:S(2)}, u32[]{:S(2)}) async-start(bf16[2,128,768]{2,1,0:T(8,128)(2,1)} %bitcast.15), calls=%async_computation.2 | async-start | bytes 786432 | tf_op jit(solution)/shard_map/all_to_all | solution.py:70
  42.1 7.5 %copy-start.1 = (bf16[1,256,768]{2,1,0:T(8,128)(2,1)S(1)}, bf16[1,256,768]{2,1,0:T(8,128)(2,1)}, u32[]{:S(2)}) copy-start(bf16[1,256,768]{2,1,0:T(8,128)(2,1)} %param.8) | copy-start | bytes 1179652
  49.9 136.2 %collective-permute-start = (bf16[1,2,768]{2,1,0:T(2,128)(2,1)S(1)}, bf16[1,2,768]{2,1,0:T(2,128)(2,1)S(1)}, u32[]{:S(2)}, u32[]{:S(2)}) collective-permute-start(bf16[1,2,768]{2,1,0:T(2,128)(2,1)S(1)} %get-tuple-element.3), channel_id=1, source_target_pairs={{1,0},{3,2},{5,4},{7,6},{9,8},{11,10},{13,12},{15,14},{17,16},{19,... | collective-permute-start | bytes 9224 | tf_op jit(solution)/shard_map/ppermute | solution.py:16
  51.2 139.2 %collective-permute-start.1 = (bf16[1,2,768]{2,1,0:T(2,128)(2,1)S(1)}, bf16[1,2,768]{2,1,0:T(2,128)(2,1)S(1)}, u32[]{:S(2)}, u32[]{:S(2)}) collective-permute-start(bf16[1,2,768]{2,1,0:T(2,128)(2,1)S(1)} %get-tuple-element.2), channel_id=1, source_target_pairs={{0,1},{2,3},{4,5},{6,7},{8,9},{10,11},{12,13},{14,15},{16,17},{18,... | collective-permute-start | bytes 9224 | tf_op jit(solution)/shard_map/ppermute | solution.py:15
  186.1 3.9 %copy-start.2 = (bf16[5,768,768]{2,1,0:T(8,128)(2,1)S(1)}, bf16[5,768,768]{2,1,0:T(8,128)(2,1)}, u32[]{:S(2)}) copy-start(bf16[5,768,768]{2,1,0:T(8,128)(2,1)} %all-gather.2.cloned.1.call-done) | copy-start | bytes 17694724
Sparse Core Ops, SparseCore 0:
  25.7 157.0 all-reduce.1
Sparse Core Ops, SparseCore 1:
  28.3 63.6 all-gather.1
